TPU v7x, 256 devices: a whole 4x4x8 slice. The times are simulated.
256 devices in a mesh: lat: 16 (over x, y_hi, core), lon: 16 (over y_lo, z).
Axes of the slice: x: 4, y: 4 (y_hi: 2, y_lo: 2; y = y_hi * 2 + y_lo), z: 8, core: 2. Of those that a mesh axis runs over, the one named last changes fastest.
Arguments:
- feature: bfloat16 [512, 512, 384], P('lat', 'lon'), may hold values from -6 to 6
- coverage: int32 [512, 512], P('lat', 'lon'), may hold values 0 or 1
- band_rows: int32 [16], replicated, may hold values from 3 to 32, as said below
- depth_weight: bfloat16 [7, 7, 384], replicated, may hold values from -0.875 to 0.875
- norm_gain: float32 [384], replicated, may hold values from 0.25 to 1.75
- norm_shift: float32 [384], replicated, may hold values from -3 to 3
- up_weight: bfloat16 [384, 1536], P('lon'), may hold values from -0.3125 to 0.3125
- up_bias: float32 [1536], replicated, may hold values from -3 to 3
- down_weight: bfloat16 [1536, 384], P('lon'), may hold values from -0.15625 to 0.15625
- down_bias: float32 [384], replicated, may hold values from -3 to 3
- layer_scale: float32 [384], replicated, may hold values from 0.3 to 1.5
- cotangent: bfloat16 [512, 512, 384], P('lat', 'lon'), may hold values from -6 to 6
Outputs:
- block_out: bfloat16 [512, 512, 384], P('lat', 'lon')
- grad_in: bfloat16 [512, 512, 384], P('lat', 'lon')
- grad_up: float32 [384, 1536], P('lon')
- grad_down: float32 [1536, 384], P('lon')
- grad_depth: float32 [7, 7, 384], replicated
Inputs may be any that keep to these rules, and one draw needn't show every extreme that they name: `band_rows`: every band has 3 or more rows, the bands' rows sum to 256, and one band has exactly 32.
All inputs are finite; a program needn't handle non-finite values. No bound on the sum of `coverage` on one device may be relied on, other than what follows from the above.
Results may differ from a plain program's by a relative error of at most 0.0066.
Values may be sent and summed in bfloat16 or wider, within the bound.
A program may use at most 64 MiB of HBM per device.

v0:
```python
import math
import jax
import jax.numpy as jnp
from jax import lax
from jax.sharding import PartitionSpec as P

BAND_MEAN = 16
SQRT_TWO_PI = 0.7978845608028654
CUBIC = 0.044715
EPSILON = 1e-06


def padded(array, sides, width):
    for axis, dim in sides:
        size, length = (lax.axis_size(axis), array.shape[dim])
        up = [(i, (i + 1) % size) for i in range(size)]
        down = [(j, i) for i, j in up]
        last = lax.slice_in_dim(array, length - width, length, axis=dim)
        initial = lax.slice_in_dim(array, 0, width, axis=dim)
        before = lax.ppermute(last, axis, up)
        after = lax.ppermute(initial, axis, down)
        array = jnp.concatenate([before, array, after], axis=dim)
    return array


def shifted(block, axis, distance):
    devices = range(lax.axis_size(axis))
    route = [(i - distance, i) for i in devices if i - distance in devices]
    return lax.ppermute(block, axis, route)


def smooth_gate(pre_act):
    argument = SQRT_TWO_PI * (pre_act + CUBIC * pre_act * pre_act * pre_act)
    return 0.5 * pre_act * (1.0 + jnp.tanh(argument))


def smooth_slope(pre_act):
    argument = SQRT_TWO_PI * (pre_act + CUBIC * pre_act * pre_act * pre_act)
    tangent = jnp.tanh(argument)
    return 0.5 * (1.0 + tangent) + 0.5 * pre_act * (1.0 - tangent * tangent) * SQRT_TWO_PI * (
        1.0 + 3.0 * CUBIC * pre_act * pre_act
    )


def extend(field, live_rows):
    widened = padded(field, (("lon", 1),), 3)
    last_rows = lax.dynamic_slice_in_dim(widened, live_rows - 3, 3, 0)
    from_above = shifted(last_rows, "lat", 1)
    from_below = shifted(widened[:3], "lat", -1)
    zero_rows = jnp.zeros((3,) + widened.shape[1:], widened.dtype)
    stacked = jnp.concatenate([from_above, widened, zero_rows], axis=0)
    return lax.dynamic_update_slice_in_dim(stacked, from_below, live_rows + 3, 0)


def shards(
    feature,
    coverage,
    band_rows,
    depth_weight,
    norm_gain,
    norm_shift,
    up_weight,
    up_bias,
    down_weight,
    down_bias,
    layer_scale,
    cotangent,
):
    rows_max, tile_cols, channels = feature.shape
    kernel = depth_weight.shape[0]
    live_rows = lax.dynamic_index_in_dim(band_rows, lax.axis_index("lat"), 0, keepdims=False)
    inside = jnp.arange(rows_max, dtype=jnp.int32) < live_rows
    covered = jnp.where(inside[:, None], coverage, 0).astype(jnp.bfloat16)
    masked = feature * covered[:, :, None]
    framed = extend(masked, live_rows)
    depth_out = jnp.zeros((rows_max, tile_cols, channels), jnp.float32)
    for row_off in range(kernel):
        for col_off in range(kernel):
            depth_out = depth_out + framed[
                row_off : row_off + rows_max, col_off : col_off + tile_cols
            ].astype(jnp.float32) * depth_weight[row_off, col_off].astype(jnp.float32)
    full_up, full_down = (
        lax.all_gather(up_weight, "lon", axis=0, tiled=True),
        lax.all_gather(down_weight, "lon", axis=0, tiled=True),
    )
    depth_rows = depth_out.reshape(-1, channels)
    center = jnp.mean(depth_rows, axis=-1, keepdims=True)
    offset = depth_rows - center
    scale_inv = lax.rsqrt(jnp.mean(offset * offset, axis=-1, keepdims=True) + EPSILON)
    standard = offset * scale_inv
    normed = (standard * norm_gain + norm_shift).astype(jnp.bfloat16)
    before = jnp.dot(normed, full_up, preferred_element_type=jnp.float32) + up_bias
    active = smooth_gate(before).astype(jnp.bfloat16)
    branch = jnp.dot(active, full_down, preferred_element_type=jnp.float32) + down_bias
    result = (feature.reshape(-1, channels).astype(jnp.float32) + layer_scale * branch).astype(
        jnp.bfloat16
    )
    cot_live = jnp.where(inside[:, None, None], cotangent, jnp.zeros_like(cotangent)).reshape(
        -1, channels
    )
    upstream = (layer_scale * cot_live.astype(jnp.float32)).astype(jnp.bfloat16)
    sum_down = lax.dot_general(
        active, upstream, (((0,), (0,)), ((), ())), preferred_element_type=jnp.float32
    )
    back_active = lax.dot_general(
        upstream, full_down, (((1,), (1,)), ((), ())), preferred_element_type=jnp.float32
    )
    back_before = (back_active * smooth_slope(before)).astype(jnp.bfloat16)
    sum_up = lax.dot_general(
        normed, back_before, (((0,), (0,)), ((), ())), preferred_element_type=jnp.float32
    )
    back_normed = lax.dot_general(
        back_before, full_up, (((1,), (1,)), ((), ())), preferred_element_type=jnp.float32
    )
    back_unit = back_normed * norm_gain
    back_depth = scale_inv * (
        back_unit
        - jnp.mean(back_unit, axis=-1, keepdims=True)
        - standard * jnp.mean(back_unit * standard, axis=-1, keepdims=True)
    )
    back_depth = back_depth.astype(jnp.bfloat16).reshape(rows_max, tile_cols, channels)
    framed_back = extend(back_depth, live_rows)
    spread = jnp.zeros((rows_max, tile_cols, channels), jnp.float32)
    tap_list = []
    for row_off in range(kernel):
        for col_off in range(kernel):
            spread = spread + framed_back[
                6 - row_off : 6 - row_off + rows_max, 6 - col_off : 6 - col_off + tile_cols
            ].astype(jnp.float32) * depth_weight[row_off, col_off].astype(jnp.float32)
            tap_list.append(
                jnp.sum(
                    framed[row_off : row_off + rows_max, col_off : col_off + tile_cols].astype(
                        jnp.float32
                    )
                    * back_depth.astype(jnp.float32),
                    axis=(0, 1),
                )
            )
    grad_local = (
        cotangent.astype(jnp.float32) + covered.astype(jnp.float32)[:, :, None] * spread
    ).astype(jnp.bfloat16)
    grad_in = jnp.where(inside[:, None, None], grad_local, jnp.zeros_like(grad_local))
    block_out = jnp.where(
        inside[:, None, None],
        result.reshape(rows_max, tile_cols, channels),
        jnp.zeros_like(feature),
    )
    rscale = 1.0 / math.sqrt(BAND_MEAN * lax.axis_size("lat") * tile_cols * lax.axis_size("lon"))
    tap_terms = jnp.stack(tap_list, axis=0).reshape(kernel, kernel, channels)
    grad_depth = lax.psum(tap_terms, ("lat", "lon")) * rscale
    up_part, down_part = (
        lax.psum_scatter(sum_up, "lon", scatter_dimension=0, tiled=True),
        lax.psum_scatter(sum_down, "lon", scatter_dimension=0, tiled=True),
    )
    up_part, down_part = lax.psum((up_part, down_part), "lat")
    return (block_out, grad_in, up_part * rscale, down_part * rscale, grad_depth)


def solution(mesh):
    placed = (
        P("lat", "lon", None),
        P("lat", "lon"),
        P(),
        P(),
        P(),
        P(),
        P("lon", None),
        P(),
        P("lon", None),
        P(),
        P(),
        P("lat", "lon", None),
    )
    return jax.shard_map(
        shards,
        mesh=mesh,
        in_specs=placed,
        out_specs=(
            P("lat", "lon", None),
            P("lat", "lon", None),
            P("lon", None),
            P("lon", None),
            P(),
        ),
        check_vma=False,
    )
```

profile of v0, /device:TPU:8, one launch (start us, length us, event | category | flops | bytes accessed | tf_op | source)
XLA Modules:
  0.0 711.5 jit_solution(1951065629706237876)
XLA Ops:
  8.0 1.2 dynamic_slice.10
  10.7 1.3 broadcast_multiply_fusion
  12.1 2.0 collective-permute-start
  14.1 3.9 collective-permute-start.1
  22.6 1.5 collective-permute-start.2
  24.7 1.3 collective-permute-start.3
  27.1 3.4 collective-permute-done.3
  30.9 12.5 %fusion.109 = (f32[32,32]{1,0:T(8,128)S(1)}, f32[32,32,384]{2,1,0:T(8,128)S(1)}) fusion(f32[384]{0:T(512)} %get-tuple-element.103, bf16[38,38,384]{2,1,0:T(8,128)(2,1)S(1)} %constant_dynamic-update-slice_fusion.1, f32[384]{0:T(512)} %get-tuple-element.104, f32[384]{0:T(512)S(1)} %get-tuple-element.57, f32[384]{0:T(512)S(1)} %get-tuple-element.58, ...), kind=kLoop, calls=%fused_computation.289 | loop fusion | flops 57801728 | bytes 40187392 | tf_op jit(solution)/shard_map/reduce_sum | solution.py:87
  44.2 1.2 add_convert_fusion.1
  45.4 36.1 %all-gather.3.cloned.1.call-done = bf16[384,1536]{1,0:T(8,128)(2,1)} async-done(((bf16[24,1536]{1,0:T(8,128)(2,1)}), bf16[384,1536]{1,0:T(8,128)(2,1)}) %all-gather.3.cloned.1.call-update) | async-done | bytes 1179664 | tf_op jit(solution)/shard_map/all_gather | solution.py:83
  81.5 7.8 %multiply_convert_fusion = (bf16[1024,1536]{1,0:T(8,128)(2,1)}, f32[1024,1536]{1,0:T(8,128)}) fusion(f32[1536]{0:T(1024)} %param.19, bf16[1024,384]{1,0:T(8,128)(2,1)} %add_convert_fusion.1, bf16[384,1536]{1,0:T(8,128)(2,1)} %all-gather.3.cloned.1.call-done), kind=kOutput, calls=%fused_computation.58 | convolution fusion | flops 1223688192 | bytes 11409408 | tf_op jit(solution)/shard_map/dot_general | solution.py:92
  89.3 61.2 %all-gather.5.cloned.1.call-done = bf16[1536,384]{1,0:T(8,128)(2,1)} async-done(((bf16[96,384]{1,0:T(8,128)(2,1)}), bf16[1536,384]{1,0:T(8,128)(2,1)}) %all-gather.5.cloned.1.call-update) | async-done | bytes 1179664 | tf_op jit(solution)/shard_map/all_gather | solution.py:84
  150.5 4.2 fusion.105
  157.3 5.4 fusion.6
  162.7 2.0 fusion.107
  164.8 5.0 fusion.103
  169.7 3.0 fusion.67
  172.8 4.0 fusion.85
  178.2 5.2 fusion.116
  184.6 4.7 fusion.115
  190.1 3.5 collective-permute-start.5
  193.6 2.6 collective-permute-done.4
  197.2 1.3 collective-permute-start.6
  198.5 218.1 %all-reduce.4.cloned.1.call-done = f32[7,7,384]{2,1,0:T(8,128)} async-done(((f32[7,7,384]{2,1,0:T(8,128)}), f32[7,7,384]{2,1,0:T(8,128)}) %all-reduce.4.cloned.1.call-update) | async-done | bytes 75280 | tf_op jit(solution)/shard_map/psum | solution.py:150
  416.6 1.5 broadcast_multiply_fusion.3
  418.1 1.3 collective-permute-start.7
  421.3 68.6 %reduce-scatter.5.cloned.1.call-done = f32[96,384]{1,0:T(8,128)} async-done(((f32[1536,384]{1,0:T(8,128)}), f32[96,384]{1,0:T(8,128)}) %reduce-scatter.5.cloned.1.call-update) | async-done | bytes 147472 | tf_op jit(solution)/shard_map/reduce_scatter | solution.py:153
  489.9 73.4 %reduce-scatter.3.cloned.1.call-done = f32[24,1536]{1,0:T(8,128)} async-done(((f32[384,1536]{1,0:T(8,128)}), f32[24,1536]{1,0:T(8,128)}) %reduce-scatter.3.cloned.1.call-update) | async-done | bytes 147472 | tf_op jit(solution)/shard_map/reduce_scatter | solution.py:152
  563.8 12.6 %broadcast_select_fusion = bf16[32,32,384]{2,1,0:T(8,128)(2,1)} fusion(pred[32]{0:T(512)(128)(4,1)} %copy-done.85, f32[384]{0:T(512)} %get-tuple-element.103, bf16[38,38,384]{2,1,0:T(8,128)(2,1)S(1)} %constant_dynamic-update-slice_fusion, f32[384]{0:T(512)} %get-tuple-element.104, f32[384]{0:T(512)S(1)} %copy-done.46, f32[384]{0:T(512)S(1)} %copy-done.48, ...), kind=kLoop, calls=%fused_computation.221 | loop fusion | flops 59375616 | bytes 40187424 | tf_op jit(solution)/shard_map/jit(_where)/select_n | solution.py:142
  576.3 125.2 %all-reduce.6.cloned.1.call-done = (f32[24,1536]{1,0:T(8,128)}, f32[96,384]{1,0:T(8,128)}) async-done(((f32[24,1536]{1,0:T(8,128)}, f32[96,384]{1,0:T(8,128)}), (f32[24,1536]{1,0:T(8,128)}, f32[96,384]{1,0:T(8,128)})) %all-reduce.6.cloned.1.call-update) | async-done | bytes 294928 | tf_op jit(solution)/shard_map/psum | solution.py:155
  701.5 1.6 broadcast_multiply_fusion.2
  703.1 1.6 broadcast_multiply_fusion.1
  (287 shorter events, 14.7 us)
Async XLA Ops:
  7.2 74.3 %all-gather.3.cloned.1.call-start = ((), (), s32[]{:S(2)}) async-start(), calls=%async_computation.2 | async-start | bytes 1253376 | tf_op jit(solution)/shard_map/all_gather | solution.py:83
  7.9 142.6 %all-gather.5.cloned.1.call-start = ((), (), s32[]{:S(2)}) async-start(), calls=%async_computation.3 | async-start | bytes 1253376 | tf_op jit(solution)/shard_map/all_gather | solution.py:84
  12.1 9.8 %collective-permute-start = (bf16[32,3,384]{2,1,0:T(4,128)(2,1)S(1)}, bf16[32,3,384]{2,1,0:T(4,128)(2,1)S(1)}, u32[]{:S(2)}, u32[]{:S(2)}) collective-permute-start(bf16[32,3,384]{2,1,0:T(4,128)(2,1)S(1)} %get-tuple-element.118), channel_id=1, source_target_pairs={{0,1},{1,2},{2,3},{3,4},{4,5},{5,6},{6,7},{7,8},{8,9},{9,10},{10,1... | collective-permute-start | bytes 221192 | tf_op jit(solution)/shard_map/ppermute | solution.py:20
  14.1 7.9 %collective-permute-start.1 = (bf16[32,3,384]{2,1,0:T(4,128)(2,1)S(1)}, bf16[32,3,384]{2,1,0:T(4,128)(2,1)S(1)}, u32[]{:S(2)}, u32[]{:S(2)}) collective-permute-start(bf16[32,3,384]{2,1,0:T(4,128)(2,1)S(1)} %get-tuple-element.119), channel_id=1, source_target_pairs={{1,0},{2,1},{3,2},{4,3},{5,4},{6,5},{7,6},{8,7},{9,8},{10,9},{11,1... | collective-permute-start | bytes 221192 | tf_op jit(solution)/shard_map/ppermute | solution.py:21
  18.0 398.6 %all-reduce.4.cloned.1.call-start = ((), (), s32[]{:S(2)}) async-start(), calls=%async_computation.6 | async-start | bytes 172032 | tf_op jit(solution)/shard_map/psum | solution.py:150
  22.6 3.4 collective-permute-start.2
  24.7 5.8 collective-permute-start.3
  178.2 311.8 %reduce-scatter.5.cloned.1.call-start = ((), (), s32[]{:S(2)}) async-start(), calls=%async_computation.5 | async-start | bytes 2506752 | tf_op jit(solution)/shard_map/reduce_scatter | solution.py:153
  183.4 379.9 %reduce-scatter.3.cloned.1.call-start = ((), (), s32[]{:S(2)}) async-start(), calls=%async_computation.4 | async-start | bytes 2506752 | tf_op jit(solution)/shard_map/reduce_scatter | solution.py:152
  189.3 512.2 %all-reduce.6.cloned.1.call-start = ((), (), s32[]{:S(2)}) async-start(), calls=%async_computation.7 | async-start | bytes 589824 | tf_op jit(solution)/shard_map/psum | solution.py:155
  189.4 6.8 collective-permute-start.4
  190.1 6.1 collective-permute-start.5
  196.8 366.5 %copy-start.1 = (bf16[32,32,384]{2,1,0:T(8,128)(2,1)S(1)}, bf16[32,32,384]{2,1,0:T(8,128)(2,1)}, u32[]{:S(2)}) copy-start(bf16[32,32,384]{2,1,0:T(8,128)(2,1)} %param.23) | copy-start | bytes 2359300
  196.8 366.5 %copy-start.8 = (f32[384]{0:T(512)S(1)}, f32[384]{0:T(512)}, u32[]{:S(2)}) copy-start(f32[384]{0:T(512)} %copy-done.7) | copy-start | bytes 4612
  196.8 366.5 %copy-start.10 = (f32[384]{0:T(512)S(1)}, f32[384]{0:T(512)}, u32[]{:S(2)}) copy-start(f32[384]{0:T(512)} %copy-done.9) | copy-start | bytes 4612
  196.8 366.5 %copy-start.12 = (f32[384]{0:T(512)S(1)}, f32[384]{0:T(512)}, u32[]{:S(2)}) copy-start(f32[384]{0:T(512)} %copy-done.11) | copy-start | bytes 4612
  196.9 366.5 %copy-start.14 = (f32[384]{0:T(512)S(1)}, f32[384]{0:T(512)}, u32[]{:S(2)}) copy-start(f32[384]{0:T(512)} %copy-done.13) | copy-start | bytes 4612
  196.9 366.5 %copy-start.16 = (f32[384]{0:T(512)S(1)}, f32[384]{0:T(512)}, u32[]{:S(2)}) copy-start(f32[384]{0:T(512)} %copy-done.15) | copy-start | bytes 4612
  196.9 366.5 %copy-start.18 = (f32[384]{0:T(512)S(1)}, f32[384]{0:T(512)}, u32[]{:S(2)}) copy-start(f32[384]{0:T(512)} %copy-done.17) | copy-start | bytes 4612
  196.9 366.5 %copy-start.20 = (f32[384]{0:T(512)S(1)}, f32[384]{0:T(512)}, u32[]{:S(2)}) copy-start(f32[384]{0:T(512)} %copy-done.19) | copy-start | bytes 4612
  196.9 366.5 %copy-start.22 = (f32[384]{0:T(512)S(1)}, f32[384]{0:T(512)}, u32[]{:S(2)}) copy-start(f32[384]{0:T(512)} %copy-done.21) | copy-start | bytes 4612
  196.9 366.5 %copy-start.24 = (f32[384]{0:T(512)S(1)}, f32[384]{0:T(512)}, u32[]{:S(2)}) copy-start(f32[384]{0:T(512)} %copy-done.23) | copy-start | bytes 4612
  196.9 366.5 %copy-start.26 = (f32[384]{0:T(512)S(1)}, f32[384]{0:T(512)}, u32[]{:S(2)}) copy-start(f32[384]{0:T(512)} %copy-done.25) | copy-start | bytes 4612
  196.9 366.5 %copy-start.28 = (f32[384]{0:T(512)S(1)}, f32[384]{0:T(512)}, u32[]{:S(2)}) copy-start(f32[384]{0:T(512)} %copy-done.27) | copy-start | bytes 4612
  196.9 366.5 %copy-start.30 = (f32[384]{0:T(512)S(1)}, f32[384]{0:T(512)}, u32[]{:S(2)}) copy-start(f32[384]{0:T(512)} %copy-done.29) | copy-start | bytes 4612
  196.9 366.5 %copy-start.32 = (f32[384]{0:T(512)S(1)}, f32[384]{0:T(512)}, u32[]{:S(2)}) copy-start(f32[384]{0:T(512)} %copy-done.31) | copy-start | bytes 4612
  197.0 366.5 %copy-start.34 = (f32[384]{0:T(512)S(1)}, f32[384]{0:T(512)}, u32[]{:S(2)}) copy-start(f32[384]{0:T(512)} %copy-done.33) | copy-start | bytes 4612
  197.0 366.5 %copy-start.36 = (f32[384]{0:T(512)S(1)}, f32[384]{0:T(512)}, u32[]{:S(2)}) copy-start(f32[384]{0:T(512)} %copy-done.35) | copy-start | bytes 4612
  197.0 366.5 %copy-start.38 = (f32[384]{0:T(512)S(1)}, f32[384]{0:T(512)}, u32[]{:S(2)}) copy-start(f32[384]{0:T(512)} %copy-done.37) | copy-start | bytes 4612
  197.0 366.5 %copy-start.40 = (f32[384]{0:T(512)S(1)}, f32[384]{0:T(512)}, u32[]{:S(2)}) copy-start(f32[384]{0:T(512)} %copy-done.39) | copy-start | bytes 4612
  197.2 222.2 %collective-permute-start.6 = (bf16[3,38,384]{2,1,0:T(8,128)(2,1)S(1)}, bf16[3,38,384]{2,1,0:T(8,128)(2,1)S(1)}, u32[]{:S(2)}, u32[]{:S(2)}) collective-permute-start(bf16[3,38,384]{2,1,0:T(8,128)(2,1)S(1)} %get-tuple-element.113), channel_id=1, source_target_pairs={{0,16},{16,32},{32,48},{48,64},{64,80},{80,96},{96,112},{112,128},... | collective-permute-start | bytes 262664 | tf_op jit(solution)/shard_map/ppermute | solution.py:29
  418.1 3.2 collective-permute-start.7
  (78 other events, 8612.5 us)
Sparse Core Ops, SparseCore 0:
  9.8 71.6 all-gather.2
  83.3 67.1 all-gather.4
  178.3 238.2 all-reduce.3
  419.0 70.8 reduce-scatter.4
  492.3 70.9 reduce-scatter.2
  565.9 135.5 all-reduce.5
where the time goes:
time: 712 us
  waiting for transfers between devices  590 us (83%)
  other arithmetic  51.7 us (7%)
  matrix products  29.3 us (4%)
  between operations  18.7 us (3%)
  starting transfers between devices  15.7 us (2%)
    psum x1, waiting for transfers between devices, shards(): grad_depth = lax.psum(tap_terms, ('lat', 'lon')) * rscale  218 us
    psum x1, waiting for transfers between devices, shards(): up_part, down_part = lax.psum((up_part, down_part), 'lat')  125 us
    reduce_scatter x1, waiting for transfers between devices, shards(): lax.psum_scatter(sum_up, 'lon', scatter_dimension=0, tiled=True)  73.4 us
    reduce_scatter x1, waiting for transfers between devices, shards(): lax.psum_scatter(sum_down, 'lon', scatter_dimension=0, tiled=True)  68.6 us
    all_gather x1, waiting for transfers between devices, shards(): lax.all_gather(down_weight, 'lon', axis=0, tiled=True)  61.2 us
    all_gather x1, waiting for transfers between devices, shards(): lax.all_gather(up_weight, 'lon', axis=0, tiled=True)  36.1 us
  transfers between devices with their start and end apart: 14, of which 9 were waited for; matrix products, arithmetic and copies ran while one was open for 8% of the time, Pallas kernels for 0%

commit v1 on v0

--- a/solution.py
+++ b/solution.py
@@ -80,7 +80,9 @@
                 row_off : row_off + rows_max, col_off : col_off + tile_cols
             ].astype(jnp.float32) * depth_weight[row_off, col_off].astype(jnp.float32)
     full_up, full_down = (
-        lax.all_gather(up_weight, "lon", axis=0, tiled=True),
+        jnp.concatenate(
+            lax.all_to_all(jnp.stack([up_weight] * lax.axis_size("lon")), "lon", 0, 0), axis=0
+        ),
         lax.all_gather(down_weight, "lon", axis=0, tiled=True),
     )
     depth_rows = depth_out.reshape(-1, channels)

time: 712 us -> 655 us (0.920)
  waiting for transfers between devices: 590 us -> 519 us
    all_gather x1, waiting for transfers between devices: 61.2 us -> 19.7 us  [shards(): lax.all_gather(down_weight, 'lon', axis=0, tiled=True)]
    all_gather x1 -> x0, waiting for transfers between devices: 36.1 us -> none  [shards(): lax.all_gather(up_weight, 'lon', axis=0, tiled=True)]
    all_to_all x0 -> x1, starting transfers between devices: none -> 7.34 us  [shards(): lax.all_to_all(jnp.stack([up_weight] * lax.axis_size('lon')), 'lon', 0, 0)]
  transfers between devices with their start and end apart: 14 -> 14, of which waited for: 9 -> 9; matrix products, arithmetic and copies ran while one was open for 8% -> 9% of each run, Pallas kernels for 0% -> 0%
where the time goes in v1:
time: 655 us; the launch traced here: 654 us
  waiting for transfers between devices  519 us (79%)
  other arithmetic  53.2 us (8%)
  matrix products  32.1 us (5%)
  starting transfers between devices  22.8 us (3%)
  between operations  18.3 us (3%)
  local copies, waits for them, and re-layouts  8.24 us (1%)
    psum x1, waiting for transfers between devices, shards(): grad_depth = lax.psum(tap_terms, ('lat', 'lon')) * rscale  219 us
    psum x1, waiting for transfers between devices, shards(): up_part, down_part = lax.psum((up_part, down_part), 'lat')  125 us
    reduce_scatter x1, waiting for transfers between devices, shards(): lax.psum_scatter(sum_up, 'lon', scatter_dimension=0, tiled=True)  73.6 us
    reduce_scatter x1, waiting for transfers between devices, shards(): lax.psum_scatter(sum_down, 'lon', scatter_dimension=0, tiled=True)  68.7 us
    all_gather x1, waiting for transfers between devices, shards(): lax.all_gather(down_weight, 'lon', axis=0, tiled=True)  19.7 us
  transfers between devices with their start and end apart: 14, of which 9 were waited for; matrix products, arithmetic and copies ran while one was open for 9% of the time, Pallas kernels for 0%

profile of v1, /device:TPU:8, one launch (start us, length us, event | category | flops | bytes accessed | tf_op | source)
XLA Modules:
  0.0 653.8 jit_solution(3388396134509071848)
XLA Ops:
  11.1 1.3 broadcast_multiply_fusion
  12.5 2.0 collective-permute-start
  14.5 3.9 collective-permute-start.1
  19.6 7.3 %all-to-all-start = ((bf16[16,24,1536]{2,1,0:T(8,128)(2,1)}), bf16[16,24,1536]{2,1,0:T(8,128)(2,1)}, u32[]{:S(2)}, u32[]{:S(2)}) async-start(bf16[16,24,1536]{2,1,0:T(8,128)(2,1)} %stack.169), calls=%async_computation | async-start | bytes 2359296 | tf_op jit(solution)/shard_map/all_to_all | solution.py:84
  31.4 1.3 collective-permute-start.2
  33.3 1.3 collective-permute-start.3
  35.7 3.3 collective-permute-done.3
  39.4 12.5 %fusion.109 = (f32[32,32]{1,0:T(8,128)S(1)}, f32[32,32,384]{2,1,0:T(8,128)S(1)}) fusion(f32[384]{0:T(512)} %get-tuple-element.103, bf16[38,38,384]{2,1,0:T(8,128)(2,1)S(1)} %constant_dynamic-update-slice_fusion.1, f32[384]{0:T(512)} %get-tuple-element.104, f32[384]{0:T(512)S(1)} %get-tuple-element.57, f32[384]{0:T(512)S(1)} %get-tuple-element.58, ...), kind=kLoop, calls=%fused_computation.290 | loop fusion | flops 57801728 | bytes 40187392 | tf_op jit(solution)/shard_map/reduce_sum | solution.py:89
  54.9 6.1 all-to-all-done
  61.0 7.9 %multiply_convert_fusion = (bf16[1024,1536]{1,0:T(8,128)(2,1)}, f32[1024,1536]{1,0:T(8,128)}) fusion(f32[1536]{0:T(1024)} %param.19, bf16[1024,384]{1,0:T(8,128)(2,1)} %bitcast.86, bf16[384,1536]{1,0:T(8,128)(2,1)} %bitcast.3), kind=kOutput, calls=%fused_computation.58 | convolution fusion | flops 1223688192 | bytes 11409408 | tf_op jit(solution)/shard_map/dot_general | solution.py:94
  68.9 19.7 %all-gather.2.cloned.1.call-done = bf16[1536,384]{1,0:T(8,128)(2,1)} async-done(((bf16[96,384]{1,0:T(8,128)(2,1)}), bf16[1536,384]{1,0:T(8,128)(2,1)}) %all-gather.2.cloned.1.call-update) | async-done | bytes 1179664 | tf_op jit(solution)/shard_map/all_gather | solution.py:86
  88.6 4.2 fusion.105
  92.9 1.7 broadcast_select_fusion.1
  96.1 5.4 fusion.6
  101.5 4.7 fusion.107
  106.3 4.9 fusion.103
  111.2 3.0 fusion.67
  114.3 4.0 fusion.85
  119.7 5.2 fusion.116
  126.0 4.7 fusion.115
  131.1 4.1 collective-permute-start.5
  135.1 2.6 collective-permute-done.4
  138.7 1.3 collective-permute-start.6
  140.0 218.8 %all-reduce.4.cloned.1.call-done = f32[7,7,384]{2,1,0:T(8,128)} async-done(((f32[7,7,384]{2,1,0:T(8,128)}), f32[7,7,384]{2,1,0:T(8,128)}) %all-reduce.4.cloned.1.call-update) | async-done | bytes 75280 | tf_op jit(solution)/shard_map/psum | solution.py:152
  358.8 1.5 broadcast_multiply_fusion.3
  360.3 1.3 collective-permute-start.7
  363.5 68.7 %reduce-scatter.5.cloned.1.call-done = f32[96,384]{1,0:T(8,128)} async-done(((f32[1536,384]{1,0:T(8,128)}), f32[96,384]{1,0:T(8,128)}) %reduce-scatter.5.cloned.1.call-update) | async-done | bytes 147472 | tf_op jit(solution)/shard_map/reduce_scatter | solution.py:155
  432.2 73.6 %reduce-scatter.3.cloned.1.call-done = f32[24,1536]{1,0:T(8,128)} async-done(((f32[384,1536]{1,0:T(8,128)}), f32[24,1536]{1,0:T(8,128)}) %reduce-scatter.3.cloned.1.call-update) | async-done | bytes 147472 | tf_op jit(solution)/shard_map/reduce_scatter | solution.py:154
  506.2 13.1 %broadcast_select_fusion = bf16[32,32,384]{2,1,0:T(8,128)(2,1)} fusion(pred[32]{0:T(512)(128)(4,1)} %iota_compare_fusion, f32[384]{0:T(512)} %get-tuple-element.103, bf16[38,38,384]{2,1,0:T(8,128)(2,1)S(1)} %constant_dynamic-update-slice_fusion, f32[384]{0:T(512)} %get-tuple-element.104, f32[384]{0:T(512)S(1)} %copy-done.42, f32[384]{0:T(512)S(1)} %copy-done.44, ...), kind=kLoop, calls=%fused_computation.222 | loop fusion | flops 59375616 | bytes 40187424 | tf_op jit(solution)/shard_map/jit(_where)/select_n | solution.py:144
  519.3 124.8 %all-reduce.6.cloned.1.call-done = (f32[24,1536]{1,0:T(8,128)}, f32[96,384]{1,0:T(8,128)}) async-done(((f32[24,1536]{1,0:T(8,128)}, f32[96,384]{1,0:T(8,128)}), (f32[24,1536]{1,0:T(8,128)}, f32[96,384]{1,0:T(8,128)})) %all-reduce.6.cloned.1.call-update) | async-done | bytes 294928 | tf_op jit(solution)/shard_map/psum | solution.py:157
  644.1 1.6 broadcast_multiply_fusion.2
  645.7 1.6 broadcast_multiply_fusion.1
  (289 shorter events, 18.1 us)
Async XLA Ops:
  7.2 81.4 %all-gather.2.cloned.1.call-start = ((), (), s32[]{:S(2)}) async-start(), calls=%async_computation.3 | async-start | bytes 1253376 | tf_op jit(solution)/shard_map/all_gather | solution.py:86
  12.5 18.2 %collective-permute-start = (bf16[32,3,384]{2,1,0:T(4,128)(2,1)S(1)}, bf16[32,3,384]{2,1,0:T(4,128)(2,1)S(1)}, u32[]{:S(2)}, u32[]{:S(2)}) collective-permute-start(bf16[32,3,384]{2,1,0:T(4,128)(2,1)S(1)} %get-tuple-element.119), channel_id=1, source_target_pairs={{0,1},{1,2},{2,3},{3,4},{4,5},{5,6},{6,7},{7,8},{8,9},{9,10},{10,1... | collective-permute-start | bytes 221192 | tf_op jit(solution)/shard_map/ppermute | solution.py:20
  14.5 16.2 %collective-permute-start.1 = (bf16[32,3,384]{2,1,0:T(4,128)(2,1)S(1)}, bf16[32,3,384]{2,1,0:T(4,128)(2,1)S(1)}, u32[]{:S(2)}, u32[]{:S(2)}) collective-permute-start(bf16[32,3,384]{2,1,0:T(4,128)(2,1)S(1)} %get-tuple-element.120), channel_id=1, source_target_pairs={{1,0},{2,1},{3,2},{4,3},{5,4},{6,5},{7,6},{8,7},{9,8},{10,9},{11,1... | collective-permute-start | bytes 221192 | tf_op jit(solution)/shard_map/ppermute | solution.py:21
  19.6 41.5 %all-to-all-start = ((bf16[16,24,1536]{2,1,0:T(8,128)(2,1)}), bf16[16,24,1536]{2,1,0:T(8,128)(2,1)}, u32[]{:S(2)}, u32[]{:S(2)}) async-start(bf16[16,24,1536]{2,1,0:T(8,128)(2,1)} %stack.169), calls=%async_computation | async-start | bytes 2359296 | tf_op jit(solution)/shard_map/all_to_all | solution.py:84
  26.9 331.9 %all-reduce.4.cloned.1.call-start = ((), (), s32[]{:S(2)}) async-start(), calls=%async_computation.6 | async-start | bytes 172032 | tf_op jit(solution)/shard_map/psum | solution.py:152
  31.4 3.3 collective-permute-start.2
  33.3 5.7 collective-permute-start.3
  119.7 312.6 %reduce-scatter.5.cloned.1.call-start = ((), (), s32[]{:S(2)}) async-start(), calls=%async_computation.5 | async-start | bytes 2506752 | tf_op jit(solution)/shard_map/reduce_scatter | solution.py:155
  124.9 380.9 %reduce-scatter.3.cloned.1.call-start = ((), (), s32[]{:S(2)}) async-start(), calls=%async_computation.4 | async-start | bytes 2506752 | tf_op jit(solution)/shard_map/reduce_scatter | solution.py:154
  130.8 513.3 %all-reduce.6.cloned.1.call-start = ((), (), s32[]{:S(2)}) async-start(), calls=%async_computation.7 | async-start | bytes 589824 | tf_op jit(solution)/shard_map/psum | solution.py:157
  130.9 6.8 %collective-permute-start.4 = (bf16[32,3,384]{2,1,0:T(4,128)(2,1)S(1)}, bf16[32,3,384]{2,1,0:T(4,128)(2,1)S(1)}, u32[]{:S(2)}, u32[]{:S(2)}) collective-permute-start(bf16[32,3,384]{2,1,0:T(4,128)(2,1)S(1)} %get-tuple-element.117), channel_id=1, source_target_pairs={{0,1},{1,2},{2,3},{3,4},{4,5},{5,6},{6,7},{7,8},{8,9},{9,10},{10,1... | collective-permute-start | bytes 221192 | tf_op jit(solution)/shard_map/ppermute | solution.py:20
  131.1 6.7 %collective-permute-start.5 = (bf16[32,3,384]{2,1,0:T(4,128)(2,1)S(1)}, bf16[32,3,384]{2,1,0:T(4,128)(2,1)S(1)}, u32[]{:S(2)}, u32[]{:S(2)}) collective-permute-start(bf16[32,3,384]{2,1,0:T(4,128)(2,1)S(1)} %get-tuple-element.118), channel_id=1, source_target_pairs={{1,0},{2,1},{3,2},{4,3},{5,4},{6,5},{7,6},{8,7},{9,8},{10,9},{11,1... | collective-permute-start | bytes 221192 | tf_op jit(solution)/shard_map/ppermute | solution.py:21
  138.3 367.6 %copy-start.1 = (bf16[32,32,384]{2,1,0:T(8,128)(2,1)S(1)}, bf16[32,32,384]{2,1,0:T(8,128)(2,1)}, u32[]{:S(2)}) copy-start(bf16[32,32,384]{2,1,0:T(8,128)(2,1)} %param.23) | copy-start | bytes 2359300
  138.3 367.5 %copy-start.8 = (f32[384]{0:T(512)S(1)}, f32[384]{0:T(512)}, u32[]{:S(2)}) copy-start(f32[384]{0:T(512)} %copy-done.7) | copy-start | bytes 4612
  138.3 367.5 %copy-start.10 = (f32[384]{0:T(512)S(1)}, f32[384]{0:T(512)}, u32[]{:S(2)}) copy-start(f32[384]{0:T(512)} %copy-done.9) | copy-start | bytes 4612
  138.3 367.5 %copy-start.12 = (f32[384]{0:T(512)S(1)}, f32[384]{0:T(512)}, u32[]{:S(2)}) copy-start(f32[384]{0:T(512)} %copy-done.11) | copy-start | bytes 4612
  138.3 367.5 %copy-start.14 = (f32[384]{0:T(512)S(1)}, f32[384]{0:T(512)}, u32[]{:S(2)}) copy-start(f32[384]{0:T(512)} %copy-done.13) | copy-start | bytes 4612
  138.3 367.5 %copy-start.16 = (f32[384]{0:T(512)S(1)}, f32[384]{0:T(512)}, u32[]{:S(2)}) copy-start(f32[384]{0:T(512)} %copy-done.15) | copy-start | bytes 4612
  138.3 367.5 %copy-start.18 = (f32[384]{0:T(512)S(1)}, f32[384]{0:T(512)}, u32[]{:S(2)}) copy-start(f32[384]{0:T(512)} %copy-done.17) | copy-start | bytes 4612
  138.4 367.5 %copy-start.20 = (f32[384]{0:T(512)S(1)}, f32[384]{0:T(512)}, u32[]{:S(2)}) copy-start(f32[384]{0:T(512)} %copy-done.19) | copy-start | bytes 4612
  138.4 367.5 %copy-start.22 = (f32[384]{0:T(512)S(1)}, f32[384]{0:T(512)}, u32[]{:S(2)}) copy-start(f32[384]{0:T(512)} %copy-done.21) | copy-start | bytes 4612
  138.4 367.5 %copy-start.24 = (f32[384]{0:T(512)S(1)}, f32[384]{0:T(512)}, u32[]{:S(2)}) copy-start(f32[384]{0:T(512)} %copy-done.23) | copy-start | bytes 4612
  138.4 367.5 %copy-start.26 = (f32[384]{0:T(512)S(1)}, f32[384]{0:T(512)}, u32[]{:S(2)}) copy-start(f32[384]{0:T(512)} %copy-done.25) | copy-start | bytes 4612
  138.4 367.5 %copy-start.28 = (f32[384]{0:T(512)S(1)}, f32[384]{0:T(512)}, u32[]{:S(2)}) copy-start(f32[384]{0:T(512)} %copy-done.27) | copy-start | bytes 4612
  138.4 367.5 %copy-start.30 = (f32[384]{0:T(512)S(1)}, f32[384]{0:T(512)}, u32[]{:S(2)}) copy-start(f32[384]{0:T(512)} %copy-done.29) | copy-start | bytes 4612
  138.4 367.5 %copy-start.32 = (f32[384]{0:T(512)S(1)}, f32[384]{0:T(512)}, u32[]{:S(2)}) copy-start(f32[384]{0:T(512)} %copy-done.31) | copy-start | bytes 4612
  138.4 367.5 %copy-start.34 = (f32[384]{0:T(512)S(1)}, f32[384]{0:T(512)}, u32[]{:S(2)}) copy-start(f32[384]{0:T(512)} %copy-done.33) | copy-start | bytes 4612
  138.4 367.5 %copy-start.36 = (f32[384]{0:T(512)S(1)}, f32[384]{0:T(512)}, u32[]{:S(2)}) copy-start(f32[384]{0:T(512)} %copy-done.35) | copy-start | bytes 4612
  138.4 367.5 %copy-start.38 = (f32[384]{0:T(512)S(1)}, f32[384]{0:T(512)}, u32[]{:S(2)}) copy-start(f32[384]{0:T(512)} %copy-done.37) | copy-start | bytes 4612
  138.5 367.5 %copy-start.40 = (f32[384]{0:T(512)S(1)}, f32[384]{0:T(512)}, u32[]{:S(2)}) copy-start(f32[384]{0:T(512)} %copy-done.39) | copy-start | bytes 4612
  138.7 222.9 %collective-permute-start.6 = (bf16[3,38,384]{2,1,0:T(8,128)(2,1)S(1)}, bf16[3,38,384]{2,1,0:T(8,128)(2,1)S(1)}, u32[]{:S(2)}, u32[]{:S(2)}) collective-permute-start(bf16[3,38,384]{2,1,0:T(8,128)(2,1)S(1)} %get-tuple-element.114), channel_id=1, source_target_pairs={{0,16},{16,32},{32,48},{48,64},{64,80},{80,96},{96,112},{112,128},... | collective-permute-start | bytes 262664 | tf_op jit(solution)/shard_map/ppermute | solution.py:29
  360.3 3.2 collective-permute-start.7
  (79 other events, 8587.7 us)
Sparse Core Ops, SparseCore 0:
  9.8 78.7 all-gather.1
  119.8 238.9 all-reduce.3
  361.4 70.8 reduce-scatter.4
  434.6 71.1 reduce-scatter.2
  508.4 135.7 all-reduce.5
